TPU v7x, 128 devices: a whole 4x4x4 slice. The times are simulated.
128 devices in a mesh: seq: 16 (over z, y), tensor: 8 (over x, core).
Axes of the slice: x: 4, y: 4, z: 4, core: 2. Of those that a mesh axis runs over, the one named last changes fastest.
Arguments:
- tokens: bfloat16 [256, 4, 3072], P('seq'), may hold values from -6 to 6
- lengths: int32 [256], replicated, may hold values from 1 to 16384, as said below
- page_request: int32 [2048], P('seq'), may hold values from 0 to 255, as said below
- page_block: int32 [2048], P('seq'), may hold values from 0 to 128, as said below
- k_cache: bfloat16 [2048, 8, 128, 128], P('seq', 'tensor'), may hold values from -330 to 330
- v_cache: bfloat16 [2048, 8, 128, 128], P('seq', 'tensor'), may hold values from -6 to 6
- attn_gain: bfloat16 [3072], replicated, may hold values from 0.099609375 to 1.8984375
- w_query: bfloat16 [3072, 3072], P(None, 'tensor'), may hold values from -0.109375 to 0.109375
- w_key: bfloat16 [3072, 1024], P(None, 'tensor'), may hold values from -0.109375 to 0.109375
- w_value: bfloat16 [3072, 1024], P(None, 'tensor'), may hold values from -0.109375 to 0.109375
- w_out: bfloat16 [3072, 3072], P('tensor'), may hold values from -0.109375 to 0.109375
- mlp_gain: bfloat16 [3072], replicated, may hold values from 0.099609375 to 1.8984375
- w_gate: bfloat16 [3072, 4096], P(None, 'tensor'), may hold values from -0.109375 to 0.109375
- w_up: bfloat16 [3072, 4096], P(None, 'tensor'), may hold values from -0.109375 to 0.109375
- w_down: bfloat16 [4096, 3072], P('tensor'), may hold values from -0.09375 to 0.09375
Outputs:
- layer_out: bfloat16 [256, 4, 3072], P('seq', None, 'tensor')
Inputs may be any that keep to these rules, and one draw needn't show every extreme that they name: `lengths`: A request r whose index is a multiple of 32 has a long cache, within 128 tokens of 16384; the others have at most 511. Request 0 has exactly 16384. `page_request`: each pair of a long request and a page number below 128, or of a short request and a page number below 4, appears in exactly one slot; slots of pages at or beyond a request's length hold no used position. A short request's pages lie in the slots of the seq index that holds its tokens. `page_block`: slots of page number 128 hold no used position.
All inputs are finite; a program needn't handle non-finite values.
Results may differ from a plain program's by a relative error of at most 0.012.
Values may be sent and summed in bfloat16 or wider, within the bound.
No kernel may reach another device: no remote copies, remote signals or barrier semaphores. Data moves between devices by JAX's collectives and lax.ppermute only.
A program may use at most 128 MiB of HBM per device.

v0:
```python
import math
import jax
import jax.numpy as jnp
from jax import lax
from jax.sharding import PartitionSpec as P

EPSILON = 1e-05
NEGATIVE = -1e30
ROPE_BASE = 500000.0


def rms_norm(values, gains):
    mean_square = jnp.mean(values * values, axis=-1, keepdims=True)
    return values * lax.rsqrt(mean_square + EPSILON) * gains.astype(jnp.float32)


def rotary(values, position):
    head_width = values.shape[-1]
    half_width = head_width // 2
    inverse = 1.0 / ROPE_BASE ** (jnp.arange(half_width, dtype=jnp.float32) * 2.0 / head_width)
    angle = position.astype(jnp.float32)[..., None, None] * inverse
    cosine = jnp.cos(angle)
    sine_table = jnp.sin(angle)
    front_half = values[..., :half_width]
    back_half = values[..., half_width:]
    return jnp.concatenate(
        [
            front_half * cosine - back_half * sine_table,
            back_half * cosine + front_half * sine_table,
        ],
        axis=-1,
    )


def per_device(
    tokens,
    lengths,
    page_request,
    page_block,
    k_cache,
    v_cache,
    attn_gain,
    w_query,
    w_key,
    w_value,
    w_out,
    mlp_gain,
    w_gate,
    w_up,
    w_down,
):
    req_dev, fresh_count, model_width = tokens.shape
    head_dim = k_cache.shape[-1]
    page_len = k_cache.shape[2]
    kv_local = k_cache.shape[1]
    group_size = w_query.shape[1] // (kv_local * head_dim)
    lanes = fresh_count * group_size
    row_count = req_dev * fresh_count
    score_scale = 1.0 / math.sqrt(head_dim)
    seq_index = lax.axis_index("seq")
    home_row = seq_index * req_dev
    own_length = lax.dynamic_slice_in_dim(lengths, home_row, req_dev)
    position = own_length[:, None] + jnp.arange(fresh_count, dtype=jnp.int32)[None, :]
    values_in = tokens.astype(jnp.float32)
    normed_in = rms_norm(values_in, attn_gain).astype(jnp.bfloat16).reshape(row_count, model_width)
    queries = jnp.dot(normed_in, w_query, preferred_element_type=jnp.float32).reshape(
        req_dev, fresh_count, kv_local * group_size, head_dim
    )
    queries = rotary(queries, position).astype(jnp.bfloat16)
    queries = queries.reshape(req_dev, fresh_count, kv_local, group_size, head_dim).transpose(
        0, 2, 1, 3, 4
    )
    queries = queries.reshape(req_dev, kv_local, lanes, head_dim)
    key_new = jnp.dot(normed_in, w_key, preferred_element_type=jnp.float32).reshape(
        req_dev, fresh_count, kv_local, head_dim
    )
    key_new = rotary(key_new, position).astype(jnp.bfloat16).transpose(0, 2, 1, 3)
    value_new = jnp.dot(normed_in, w_value, preferred_element_type=jnp.float32).astype(jnp.bfloat16)
    value_new = value_new.reshape(req_dev, fresh_count, kv_local, head_dim).transpose(0, 2, 1, 3)
    requests = lengths.shape[0]
    owner_member = page_request[:, None] == jnp.arange(requests, dtype=jnp.int32)[None, :]
    owner_length = jnp.sum(jnp.where(owner_member, lengths[None, :], 0), axis=1)
    offsets = jnp.arange(page_len, dtype=jnp.int32)
    is_valid = page_block[:, None] * page_len + offsets[None, :] < owner_length[:, None]
    fresh_scores = (
        jnp.einsum("rhqd,rhsd->rhqs", queries, key_new, preferred_element_type=jnp.float32)
        * score_scale
    )
    causal = (jnp.arange(lanes, dtype=jnp.int32) // group_size)[:, None] >= jnp.arange(
        fresh_count, dtype=jnp.int32
    )[None, :]
    fresh_scores = jnp.where(causal[None, None], fresh_scores, NEGATIVE)
    fresh_top = jnp.max(fresh_scores, axis=-1)
    every_query = lax.all_gather(
        queries.reshape(req_dev, kv_local * lanes * head_dim), "seq", axis=0, tiled=True
    )
    chosen = every_query[page_request].reshape(-1, kv_local, lanes, head_dim)
    scores = (
        jnp.einsum("phqd,phkd->phqk", chosen, k_cache, preferred_element_type=jnp.float32)
        * score_scale
    )
    scores = jnp.where(is_valid[:, None, None, :], scores, NEGATIVE)
    page_max = jnp.max(scores, axis=-1)
    cache_max = jnp.max(
        jnp.where(owner_member[:, :, None, None], page_max[:, None], NEGATIVE), axis=0
    )
    own_max = jnp.maximum(lax.dynamic_slice_in_dim(cache_max, home_row, req_dev, 0), fresh_top)
    candidate = lax.dynamic_update_slice_in_dim(cache_max, own_max, home_row, 0)
    row_max = lax.pmax(candidate, "seq")
    page_ref = jnp.sum(jnp.where(owner_member[:, :, None, None], row_max[None], 0.0), axis=1)
    weights = jnp.where(
        is_valid[:, None, None, :], jnp.exp(scores - page_ref[..., None]), 0.0
    ).astype(jnp.bfloat16)
    page_total = jnp.sum(weights.astype(jnp.float32), axis=-1)
    page_sum = jnp.einsum("phqk,phkd->phqd", weights, v_cache, preferred_element_type=jnp.float32)
    member_float = owner_member.astype(jnp.float32)
    slot_total = jnp.einsum(
        "pr,phq->rhq", member_float, page_total, precision=lax.Precision.HIGHEST
    )
    slot_summed = jnp.einsum(
        "pr,phqd->rhqd", member_float, page_sum, precision=lax.Precision.HIGHEST
    )
    total_all, summed_all = lax.psum((slot_total, slot_summed), "seq")
    own_total = lax.dynamic_slice_in_dim(total_all, home_row, req_dev, 0)
    own_summed = lax.dynamic_slice_in_dim(summed_all, home_row, req_dev, 0)
    own_ref = lax.dynamic_slice_in_dim(row_max, home_row, req_dev, 0)
    fresh_weights = jnp.where(
        causal[None, None], jnp.exp(fresh_scores - own_ref[..., None]), 0.0
    ).astype(jnp.bfloat16)
    own_total = own_total + jnp.sum(fresh_weights.astype(jnp.float32), axis=-1)
    own_summed = own_summed + jnp.einsum(
        "rhqs,rhsd->rhqd", fresh_weights, value_new, preferred_element_type=jnp.float32
    )
    attended = (own_summed / own_total[..., None]).astype(jnp.bfloat16)
    attended = attended.reshape(req_dev, kv_local, fresh_count, group_size, head_dim).transpose(
        0, 2, 1, 3, 4
    )
    attended = attended.reshape(row_count, kv_local * group_size * head_dim)
    partial_value = jnp.dot(attended, w_out, preferred_element_type=jnp.float32)
    flat_input = values_in.reshape(row_count, model_width)
    col_count = model_width // lax.axis_size("tensor")
    col_start = lax.axis_index("tensor") * col_count
    attn_sum = lax.psum(partial_value, "tensor")
    residual = (flat_input + attn_sum).astype(jnp.bfloat16)
    normed = rms_norm(residual.astype(jnp.float32), mlp_gain).astype(jnp.bfloat16)
    own_residual = lax.dynamic_slice_in_dim(residual, col_start, col_count, 1)
    gate_out = jnp.dot(normed, w_gate, preferred_element_type=jnp.float32)
    up_out = jnp.dot(normed, w_up, preferred_element_type=jnp.float32)
    activated = (jax.nn.silu(gate_out) * up_out).astype(jnp.bfloat16)
    down_out = jnp.dot(activated, w_down, preferred_element_type=jnp.float32)
    mlp_part = lax.psum_scatter(down_out, "tensor", scatter_dimension=1, tiled=True)
    layer_out = (own_residual.astype(jnp.float32) + mlp_part).astype(jnp.bfloat16)
    return layer_out.reshape(req_dev, fresh_count, col_count)


def solution(mesh):
    placed = (
        P("seq", None, None),
        P(),
        P("seq"),
        P("seq"),
        P("seq", "tensor", None, None),
        P("seq", "tensor", None, None),
        P(),
        P(None, "tensor"),
        P(None, "tensor"),
        P(None, "tensor"),
        P("tensor", None),
        P(),
        P(None, "tensor"),
        P(None, "tensor"),
        P("tensor", None),
    )
    return jax.shard_map(
        per_device, mesh=mesh, in_specs=placed, out_specs=P("seq", None, "tensor"), check_vma=False
    )
```

profile of v0, /device:TPU:0, one launch (start us, length us, event | category | flops | bytes accessed | tf_op | source)
XLA Modules:
  0.0 368.0 jit_solution(6125877273214239145)
XLA Ops:
  10.0 2.0 fusion.69
  20.7 4.3 %copy.81 = bf16[3072,384]{0,1:T(8,128)(2,1)} copy(bf16[3072,384]{1,0:T(8,128)(2,1)} %param.22) | data formatting | bytes 4718592 | tf_op args[7]
  25.0 2.7 fusion.18
  33.1 28.5 %all_gather.3 = bf16[256,1536]{1,0:T(8,128)(2,1)} all-gather(bf16[16,1536]{1,0:T(8,128)(2,1)} %convert_element_type.77), channel_id=1, replica_groups=mesh['seq'=16,'tensor'=8] {'seq'}, dimensions={0}, use_global_device_ids=true | all-gather | bytes 835584 | tf_op jit(solution)/shard_map/all_gather | solution.py:94
  62.3 3.2 gather_fusion
  65.5 1.9 copy.84
  67.4 2.2 copy.85
  70.4 6.3 %fusion.55 = (f32[128,12]{1,0:T(8,128)}, f32[128,12,128]{2,1,0:T(8,128)}) fusion(bf16[128,12,128]{2,1,0:T(8,128)(2,1)} %copy.85, bf16[128,1,128,128]{3,2,1,0:T(8,128)(2,1)} %param.19, pred[128,128]{1,0:T(8,128)(4,1)S(1)} %add_compare_fusion), kind=kOutput, calls=%fused_computation.94 | convolution fusion | flops 50919936 | bytes 5396480 | tf_op jit(solution)/shard_map/phqd,phkd->phqk/dot_general | solution.py:99
  84.0 72.1 %pmax.7 = f32[256,1,12]{0,2,1:T(8,128)} all-reduce(f32[256,1,12]{0,2,1:T(8,128)} %dynamic_update_slice.3), channel_id=1, replica_groups=mesh['seq'=16,'tensor'=8] {'seq'}, use_global_device_ids=true, to_apply=%region_5.6 | all-reduce | flops 3072 | bytes 24576 | tf_op jit(solution)/shard_map/pmax | solution.py:109
  156.1 1.7 select_reduce_fusion
  159.2 3.8 %fusion = f32[128,12,128]{2,1,0:T(8,128)S(1)} fusion(bf16[128,1,128,128]{3,2,1,0:T(8,128)(2,1)} %param.20, f32[128,12,128]{2,1,0:T(8,128)} %get-tuple-element.14, f32[128,12]{1,0:T(8,128)} %copy.93, pred[128,128]{1,0:T(8,128)(4,1)S(1)} %add_compare_fusion), kind=kOutput, calls=%fused_computation.1 | convolution fusion | flops 50921472 | bytes 5789696 | tf_op jit(solution)/shard_map/phqk,phkd->phqd/dot_general | solution.py:115
  163.0 2.2 convolution_bitcast_fusion
  168.4 1.9 convert_reduce_fusion
  171.2 69.6 %psum.22 = f32[256,1,12]{0,2,1:T(8,128)} all-reduce(f32[256,1,12]{0,2,1:T(8,128)S(1)} %convolution_bitcast_fusion.2), channel_id=1, replica_groups=mesh['seq'=16,'tensor'=8] {'seq'}, use_global_device_ids=true, to_apply=%region_9.10 | all-reduce | flops 3072 | bytes 24576 | tf_op jit(solution)/shard_map/psum | solution.py:123
  241.6 1.5 convolution_convert_fusion
  243.1 1.6 fusion.54
  244.8 5.9 %all-reduce.3.cloned.1.call-done = f32[256,1,12,128]{3,0,2,1:T(8,128)} async-done(((f32[256,1,12,128]{3,0,2,1:T(8,128)}), f32[256,1,12,128]{3,0,2,1:T(8,128)}) %all-reduce.3.cloned.1.call-update) | async-done | bytes 1572880 | tf_op jit(solution)/shard_map/psum | solution.py:123
  253.9 3.1 fusion.57
  258.7 59.7 %all-reduce.5.cloned.1.call-done = f32[64,3072]{1,0:T(8,128)} async-done(((f32[64,3072]{1,0:T(8,128)}), f32[64,3072]{1,0:T(8,128)}) %all-reduce.5.cloned.1.call-update) | async-done | bytes 786448 | tf_op jit(solution)/shard_map/psum | solution.py:143
  318.5 1.6 fusion.13
  320.1 3.3 fusion.29
  323.3 4.1 %fusion.11 = f32[64,3072]{1,0:T(8,128)} fusion(bf16[512,3072]{1,0:T(8,128)(2,1)S(1)} %copy-done, bf16[3072,512]{1,0:T(8,128)(2,1)} %param.28, f32[64,512]{1,0:T(8,128)} %fusion.29, bf16[64,3072]{1,0:T(8,128)(2,1)S(1)} %get-tuple-element.6, f32[3072]{0:T(1024)S(1)} %convert_element_type.87, f32[64]{0:T(128)S(1)} %add_rsqrt_fusion.1), kind=kOutput, calls=%fused_computation.12 | convolution fusion | flops 403636224 | bytes 7614720 | tf_op jit(solution)/shard_map/dot_general | solution.py:150
  327.4 31.1 %reduce-scatter.2.cloned.1.call-done = f32[64,384]{1,0:T(8,128)} async-done(((f32[64,3072]{1,0:T(8,128)}), f32[64,384]{1,0:T(8,128)}) %reduce-scatter.2.cloned.1.call-update) | async-done | bytes 98320 | tf_op jit(solution)/shard_map/reduce_scatter | solution.py:151
  358.5 1.5 add_convert_fusion.1
  (77 shorter events, 39.0 us)
Async XLA Ops:
  6.5 316.8 %copy-start = (bf16[512,3072]{1,0:T(8,128)(2,1)S(1)}, bf16[512,3072]{1,0:T(8,128)(2,1)}, u32[]{:S(2)}) copy-start(bf16[512,3072]{1,0:T(8,128)(2,1)} %param.29) | copy-start | bytes 9437188
  6.5 244.1 %all-reduce.3.cloned.1.call-start = ((), (), s32[]{:S(2)}) async-start(), calls=%async_computation.1 | async-start | bytes 3145728 | tf_op jit(solution)/shard_map/psum | solution.py:123
  6.6 12.0 %copy-start.9 = (f32[64]{0:T(128)}, f32[64]{0:T(128)S(1)}, u32[]{:S(2)}) copy-start(f32[64]{0:T(128)S(1)} %negate_power_fusion) | copy-start | bytes 772
  25.0 2.7 copy-start.2
  25.0 2.7 copy-start.3
  25.0 3.6 copy-start.11
  25.0 3.6 copy-start.6
  28.6 0.9 copy-start.8
  30.2 39.4 %copy-start.10 = (s32[128]{0:T(128)S(1)}, s32[128]{0:T(128)}, u32[]{:S(2)}) copy-start(s32[128]{0:T(128)} %param.18) | copy-start | bytes 1540
  80.7 0.6 copy-start.4
  159.2 3.8 %copy-start.7 = (s32[128]{0:T(128)S(1)}, s32[128]{0:T(128)}, u32[]{:S(2)}) copy-start(s32[128]{0:T(128)} %param.17) | copy-start | bytes 1540
  165.2 153.3 %all-reduce.5.cloned.1.call-start = ((), (), s32[]{:S(2)}) async-start(), calls=%async_computation.2 | async-start | bytes 1572864 | tf_op jit(solution)/shard_map/psum | solution.py:143
  166.9 1.5 copy-start.5
  170.3 86.8 %copy-start.1 = (bf16[16,4,3072]{2,1,0:T(4,128)(2,1)S(1)}, bf16[16,4,3072]{2,1,0:T(4,128)(2,1)}, u32[]{:S(2)}) copy-start(bf16[16,4,3072]{2,1,0:T(4,128)(2,1)} %param.15) | copy-start | bytes 1179652
  257.0 101.5 %reduce-scatter.2.cloned.1.call-start = ((), (), s32[]{:S(2)}) async-start(), calls=%async_computation.3 | async-start | bytes 884736 | tf_op jit(solution)/shard_map/reduce_scatter | solution.py:151
Sparse Core Ops, SparseCore 0:
  165.3 85.3 all-reduce.2
  257.1 61.2 all-reduce.4
  327.6 30.9 reduce-scatter.1
where the time goes:
time: 370 us; the launch traced here: 368 us
  blocking collectives  170 us (46%)
  waiting for transfers between devices  96.8 us (26%)
  matrix products  31.7 us (9%)
  local copies, waits for them, and re-layouts  29.3 us (8%)
  other arithmetic  26.6 us (7%)
  between operations  13.3 us (4%)
    pmax x1, blocking collectives, per_device(): row_max = lax.pmax(candidate, 'seq')  72.1 us
    psum x1, blocking collectives, per_device(): total_all, summed_all = lax.psum((slot_total, slot_summed), 'seq')  69.6 us
    psum x1, waiting for transfers between devices, per_device(): attn_sum = lax.psum(partial_value, 'tensor')  59.7 us
    reduce_scatter x1, waiting for transfers between devices, per_device(): lax.psum_scatter(down_out, 'tensor', scatter_dimension=1, tiled=True)  31.1 us
    all_gather x1, blocking collectives, per_device(): lax.all_gather(queries.reshape(req_dev, kv_local * lanes * head_dim), 'se...  28.5 us
  transfers between devices with their start and end apart: 3, of which 3 were waited for; matrix products, arithmetic and copies ran while one was open for 3% of the time, Pallas kernels for 0%

commit v1 on v0

--- a/solution.py
+++ b/solution.py
@@ -140,7 +140,15 @@
     flat_input = values_in.reshape(row_count, model_width)
     col_count = model_width // lax.axis_size("tensor")
     col_start = lax.axis_index("tensor") * col_count
-    attn_sum = lax.psum(partial_value, "tensor")
+    dev_count = lax.axis_size("tensor")
+    attn_sum, m_next = (partial_value, 0)
+    while 1 << m_next < dev_count:
+        row_list = []
+        for k0 in [*range(dev_count)]:
+            row_list.append((k0, k0 ^ 1 << m_next))
+        local_next = lax.ppermute(attn_sum, "tensor", row_list)
+        attn_sum = attn_sum + local_next
+        m_next = m_next + 1
     residual = (flat_input + attn_sum).astype(jnp.bfloat16)
     normed = rms_norm(residual.astype(jnp.float32), mlp_gain).astype(jnp.bfloat16)
     own_residual = lax.dynamic_slice_in_dim(residual, col_start, col_count, 1)

time: 370 us -> 350 us (0.946)
  waiting for transfers between devices: 96.8 us -> 75.4 us
  starting transfers between devices: 0.09 us -> 4.86 us
    psum x1 -> x0, waiting for transfers between devices: 59.7 us -> none  [per_device(): attn_sum = lax.psum(partial_value, 'tensor')]
    ppermute x0 -> x3, waiting for transfers between devices: none -> 36.1 us  [per_device(): local_next = lax.ppermute(attn_sum, 'tensor', row_list)]
    ppermute x0 -> x3, starting transfers between devices: none -> 4.81 us  [per_device(): local_next = lax.ppermute(attn_sum, 'tensor', row_list)]
  transfers between devices with their start and end apart: 3 -> 5, of which waited for: 3 -> 5; matrix products, arithmetic and copies ran while one was open for 3% -> 3% of each run, Pallas kernels for 0% -> 0%
where the time goes in v1:
time: 350 us; the launch traced here: 348 us
  blocking collectives  170 us (49%)
  waiting for transfers between devices  75.4 us (22%)
  matrix products  30.1 us (9%)
  other arithmetic  27.1 us (8%)
  local copies, waits for them, and re-layouts  26.6 us (8%)
  between operations  13.6 us (4%)
  starting transfers between devices  4.86 us (1%)
    pmax x1, blocking collectives, per_device(): row_max = lax.pmax(candidate, 'seq')  72.1 us
    psum x1, blocking collectives, per_device(): total_all, summed_all = lax.psum((slot_total, slot_summed), 'seq')  69.7 us
    ppermute x3, waiting for transfers between devices, per_device(): local_next = lax.ppermute(attn_sum, 'tensor', row_list)  36.1 us
    reduce_scatter x1, waiting for transfers between devices, per_device(): lax.psum_scatter(down_out, 'tensor', scatter_dimension=1, tiled=True)  31.3 us
    all_gather x1, blocking collectives, per_device(): lax.all_gather(queries.reshape(req_dev, kv_local * lanes * head_dim), 'se...  28.5 us
    psum x1, waiting for transfers between devices, per_device(): total_all, summed_all = lax.psum((slot_total, slot_summed), 'seq')  7.94 us
  transfers between devices with their start and end apart: 5, of which 5 were waited for; matrix products, arithmetic and copies ran while one was open for 3% of the time, Pallas kernels for 0%

profile of v1, /device:TPU:0, one launch (start us, length us, event | category | flops | bytes accessed | tf_op | source)
XLA Modules:
  0.0 348.0 jit_solution(10527965106581002200)
XLA Ops:
  10.0 2.0 fusion.69
  20.7 4.3 %copy.81 = bf16[3072,384]{0,1:T(8,128)(2,1)} copy(bf16[3072,384]{1,0:T(8,128)(2,1)} %param.22) | data formatting | bytes 4718592 | tf_op args[7]
  25.0 2.7 fusion.18
  33.1 28.5 %all_gather.3 = bf16[256,1536]{1,0:T(8,128)(2,1)} all-gather(bf16[16,1536]{1,0:T(8,128)(2,1)} %convert_element_type.77), channel_id=1, replica_groups=mesh['seq'=16,'tensor'=8] {'seq'}, dimensions={0}, use_global_device_ids=true | all-gather | bytes 835584 | tf_op jit(solution)/shard_map/all_gather | solution.py:94
  62.3 3.2 gather_fusion
  65.5 1.9 copy.84
  67.4 2.2 copy.85
  70.4 6.3 %fusion.55 = (f32[128,12]{1,0:T(8,128)}, f32[128,12,128]{2,1,0:T(8,128)}) fusion(bf16[128,12,128]{2,1,0:T(8,128)(2,1)} %copy.85, bf16[128,1,128,128]{3,2,1,0:T(8,128)(2,1)} %param.19, pred[128,128]{1,0:T(8,128)(4,1)S(1)} %add_compare_fusion), kind=kOutput, calls=%fused_computation.94 | convolution fusion | flops 50919936 | bytes 5396480 | tf_op jit(solution)/shard_map/phqd,phkd->phqk/dot_general | solution.py:99
  84.0 72.1 %pmax.7 = f32[256,1,12]{0,2,1:T(8,128)} all-reduce(f32[256,1,12]{0,2,1:T(8,128)} %dynamic_update_slice.3), channel_id=1, replica_groups=mesh['seq'=16,'tensor'=8] {'seq'}, use_global_device_ids=true, to_apply=%region_5.6 | all-reduce | flops 3072 | bytes 24576 | tf_op jit(solution)/shard_map/pmax | solution.py:109
  156.1 1.7 select_reduce_fusion
  159.2 3.8 %fusion = f32[128,12,128]{2,1,0:T(8,128)S(1)} fusion(bf16[128,1,128,128]{3,2,1,0:T(8,128)(2,1)} %param.20, f32[128,12,128]{2,1,0:T(8,128)} %get-tuple-element.14, f32[128,12]{1,0:T(8,128)} %copy.93, pred[128,128]{1,0:T(8,128)(4,1)S(1)} %add_compare_fusion), kind=kOutput, calls=%fused_computation.1 | convolution fusion | flops 50921472 | bytes 5789696 | tf_op jit(solution)/shard_map/phqk,phkd->phqd/dot_general | solution.py:115
  163.0 2.2 convolution_bitcast_fusion
  167.8 1.9 convert_reduce_fusion
  170.6 69.7 %psum.15 = f32[256,1,12]{0,2,1:T(8,128)S(1)} all-reduce(f32[256,1,12]{0,2,1:T(8,128)S(1)} %convolution_bitcast_fusion.2), channel_id=1, replica_groups=mesh['seq'=16,'tensor'=8] {'seq'}, use_global_device_ids=true, to_apply=%region_9.10 | all-reduce | flops 3072 | bytes 24576 | tf_op jit(solution)/shard_map/psum | solution.py:123
  242.8 7.9 %all-reduce.2.cloned.1.call-done = f32[256,1,12,128]{3,0,2,1:T(8,128)} async-done(((f32[256,1,12,128]{3,0,2,1:T(8,128)}), f32[256,1,12,128]{3,0,2,1:T(8,128)}) %all-reduce.2.cloned.1.call-update) | async-done | bytes 1572880 | tf_op jit(solution)/shard_map/psum | solution.py:123
  251.8 2.2 fusion.57
  254.1 2.3 collective-permute-done
  258.1 18.0 %collective-permute-done.1 = f32[64,3072]{1,0:T(8,128)S(1)} collective-permute-done((f32[64,3072]{1,0:T(8,128)S(1)}, f32[64,3072]{1,0:T(8,128)S(1)}, u32[]{:S(2)}, u32[]{:S(2)}) %collective-permute-start.1) | collective-permute-done | bytes 786464 | tf_op jit(solution)/shard_map/ppermute | solution.py:149
  277.1 3.1 collective-permute-start.2
  281.8 15.8 %collective-permute-done.2 = f32[64,3072]{1,0:T(8,128)} collective-permute-done((f32[64,3072]{1,0:T(8,128)}, f32[64,3072]{1,0:T(8,128)}, u32[]{:S(2)}, u32[]{:S(2)}) %collective-permute-start.2) | collective-permute-done | bytes 786464 | tf_op jit(solution)/shard_map/ppermute | solution.py:149
  297.7 1.8 fusion.13
  299.5 3.3 fusion.29
  302.8 4.1 %fusion.11 = f32[64,3072]{1,0:T(8,128)} fusion(bf16[512,3072]{1,0:T(8,128)(2,1)S(1)} %copy-done, bf16[3072,512]{1,0:T(8,128)(2,1)} %param.28, f32[64,512]{1,0:T(8,128)} %fusion.29, bf16[64,3072]{1,0:T(8,128)(2,1)S(1)} %get-tuple-element.6, f32[3072]{0:T(1024)S(1)} %convert_element_type.87, f32[64]{0:T(128)S(1)} %add_rsqrt_fusion.1), kind=kOutput, calls=%fused_computation.12 | convolution fusion | flops 403636224 | bytes 7614720 | tf_op jit(solution)/shard_map/dot_general | solution.py:158
  306.9 31.3 %reduce-scatter.2.cloned.1.call-done = f32[64,384]{1,0:T(8,128)} async-done(((f32[64,3072]{1,0:T(8,128)}), f32[64,384]{1,0:T(8,128)}) %reduce-scatter.2.cloned.1.call-update) | async-done | bytes 98320 | tf_op jit(solution)/shard_map/reduce_scatter | solution.py:159
  (80 shorter events, 42.2 us)
Async XLA Ops:
  6.5 296.3 %copy-start = (bf16[512,3072]{1,0:T(8,128)(2,1)S(1)}, bf16[512,3072]{1,0:T(8,128)(2,1)}, u32[]{:S(2)}) copy-start(bf16[512,3072]{1,0:T(8,128)(2,1)} %param.29) | copy-start | bytes 9437188
  6.5 244.2 %all-reduce.2.cloned.1.call-start = ((), (), s32[]{:S(2)}) async-start(), calls=%async_computation.1 | async-start | bytes 3145728 | tf_op jit(solution)/shard_map/psum | solution.py:123
  6.6 11.9 %copy-start.8 = (f32[64]{0:T(128)}, f32[64]{0:T(128)S(1)}, u32[]{:S(2)}) copy-start(f32[64]{0:T(128)S(1)} %negate_power_fusion) | copy-start | bytes 772
  25.0 2.7 copy-start.2
  25.0 2.7 copy-start.3
  25.0 3.6 %copy-start.10 = (s32[12]{0:T(128)S(1)}, s32[12]{0:T(128)}, u32[]{:S(2)}) copy-start(s32[12]{0:T(128)} %and_select_fusion) | copy-start | bytes 148
  25.0 3.6 %copy-start.5 = (bf16[16,4,64]{2,0,1:T(8,128)(2,1)S(1)}, bf16[16,4,64]{2,0,1:T(8,128)(2,1)}, u32[]{:S(2)}) copy-start(bf16[16,4,64]{2,0,1:T(8,128)(2,1)} %get-tuple-element.10) | copy-start | bytes 24580
  28.6 0.9 copy-start.7
  30.2 39.4 %copy-start.9 = (s32[128]{0:T(128)S(1)}, s32[128]{0:T(128)}, u32[]{:S(2)}) copy-start(s32[128]{0:T(128)} %param.18) | copy-start | bytes 1540
  80.7 0.6 copy-start.4
  159.2 3.8 %copy-start.6 = (s32[128]{0:T(128)S(1)}, s32[128]{0:T(128)}, u32[]{:S(2)}) copy-start(s32[128]{0:T(128)} %param.17) | copy-start | bytes 1540
  165.2 173.0 %reduce-scatter.2.cloned.1.call-start = ((), (), s32[]{:S(2)}) async-start(), calls=%async_computation.2 | async-start | bytes 884736 | tf_op jit(solution)/shard_map/reduce_scatter | solution.py:159
  254.0 26.2 %copy-start.1 = (bf16[16,4,3072]{2,1,0:T(4,128)(2,1)S(1)}, bf16[16,4,3072]{2,1,0:T(4,128)(2,1)}, u32[]{:S(2)}) copy-start(bf16[16,4,3072]{2,1,0:T(4,128)(2,1)} %param.15) | copy-start | bytes 1179652
  254.0 2.4 collective-permute-start
  256.5 19.7 %collective-permute-start.1 = (f32[64,3072]{1,0:T(8,128)S(1)}, f32[64,3072]{1,0:T(8,128)S(1)}, u32[]{:S(2)}, u32[]{:S(2)}) collective-permute-start(f32[64,3072]{1,0:T(8,128)S(1)} %add.130), channel_id=1, source_target_pairs={{0,2},{1,3},{2,0},{3,1},{4,6},{5,7},{6,4},{7,5},{8,10},{9,11},{10,... | collective-permute-start | bytes 2359304 | tf_op jit(solution)/shard_map/ppermute | solution.py:149
  277.1 20.5 %collective-permute-start.2 = (f32[64,3072]{1,0:T(8,128)}, f32[64,3072]{1,0:T(8,128)}, u32[]{:S(2)}, u32[]{:S(2)}) collective-permute-start(f32[64,3072]{1,0:T(8,128)} %add.131), channel_id=1, source_target_pairs={{0,4},{1,5},{2,6},{3,7},{4,0},{5,1},{6,2},{7,3},{8,12},{9,13},{10,... | collective-permute-start | bytes 2359304 | tf_op jit(solution)/shard_map/ppermute | solution.py:149
Sparse Core Ops, SparseCore 0:
  165.3 85.3 all-reduce.1
  307.0 31.1 reduce-scatter.1
